TPU v7x, 32 devices: a whole 2x2x4 slice. The times are simulated.
32 devices in a mesh: tm: 4 (over x, core), anta: 4 (over z), antb: 2 (over y).
Axes of the slice: x: 2, y: 2, z: 4, core: 2. Of those that a mesh axis runs over, the one named last changes fastest.
Arguments:
- samples: bfloat16 [2, 512, 6144], P('antb', 'anta', 'tm'), may hold values from -6 to 6
Outputs:
- correlation: float32 [256, 2, 512, 2, 512], P('tm', None, 'anta', 'antb')
All inputs are finite; a program needn't handle non-finite values.
Results may differ from a plain program's by a relative error of at most 0.0003.
Values may be sent and summed in bfloat16 or wider, within the bound.
No kernel may reach another device: no remote copies, remote signals or barrier semaphores. Data moves between devices by JAX's collectives and lax.ppermute only.
A program may use at most 128 MiB of HBM per device.

v0:
```python
import math

import jax
import jax.numpy as jnp
from jax import lax
from jax.sharding import PartitionSpec as P

ANTENNA_COUNT = 512
POLARISATION_NUM = 2
LAG_TOTAL = 256


def lag_terms(row_padded, columns, lag_start, lag_count, window_len):
    group_len = math.gcd(lag_count, 8)
    flat_cols = columns.reshape(columns.shape[1], columns.shape[2])

    def one_group(group_index):
        first_lag = lag_start + group_index * group_len
        pieces = [
            lax.dynamic_slice_in_dim(row_padded, LAG_TOTAL - first_lag - step_index, window_len, 1)
            for step_index in range(group_len)
        ]
        stacked = jnp.stack(pieces, 0)
        return jnp.einsum("kit,jt->kij", stacked, flat_cols, preferred_element_type=jnp.float32)

    grouped = lax.map(one_group, jnp.arange(lag_count // group_len, dtype=jnp.int32))
    return grouped.reshape(lag_count, row_padded.shape[0], flat_cols.shape[0])


def collect_rows(own_window):
    return lax.all_gather(own_window, "antb", axis=0, tiled=True)


def per_device(samples):
    antenna_total = samples.shape[1]
    block_len = samples.shape[2]
    tm_size = lax.axis_size("tm")
    lag_portion = LAG_TOTAL // tm_size
    full_length = block_len * tm_size
    factor = 1.0 / math.sqrt(full_length)
    lag_start = lax.axis_index("tm") * lag_portion
    col_tiles = lax.all_gather(samples, "anta", axis=1, tiled=True)
    columns = lax.all_gather(col_tiles, "tm", axis=2, tiled=True)
    own_rows = lax.dynamic_slice_in_dim(
        columns, lax.axis_index("anta") * antenna_total, antenna_total, 1
    )
    row_samples = collect_rows(own_rows)
    row_padded = jnp.pad(
        row_samples.reshape(POLARISATION_NUM * antenna_total, full_length), ((0, 0), (LAG_TOTAL, 0))
    )
    lag_group_block = lag_terms(row_padded, columns, lag_start, lag_portion, full_length)
    accumulated_sum = lag_group_block.reshape(
        lag_portion, POLARISATION_NUM, antenna_total, 1, ANTENNA_COUNT
    )
    return accumulated_sum * factor


def solution(mesh):
    return jax.shard_map(
        per_device,
        mesh=mesh,
        in_specs=(P("antb", "anta", "tm"),),
        out_specs=P("tm", None, "anta", "antb", None),
        check_vma=False,
    )
```

profile of v0, /device:TPU:0, one launch (start us, length us, event | category | flops | bytes accessed | tf_op | source)
XLA Modules:
  0.0 584.9 jit_solution(11511170079034413192)
XLA Ops:
  7.3 41.4 %all-gather.4.cloned.1.call-done = bf16[1,512,1536]{2,1,0:T(8,128)(2,1)} async-done(((bf16[1,128,1536]{2,1,0:T(8,128)(2,1)}), bf16[1,512,1536]{2,1,0:T(8,128)(2,1)}) %all-gather.4.cloned.1.call-update) | async-done | bytes 1572880 | tf_op jit(solution)/shard_map/all_gather | solution.py:42
  48.8 46.7 %all-gather.6.cloned.1.call-done = bf16[1,512,6144]{2,1,0:T(8,128)(2,1)} async-done(((bf16[1,512,1536]{2,1,0:T(8,128)(2,1)}), bf16[1,512,6144]{2,1,0:T(8,128)(2,1)}) %all-gather.6.cloned.1.call-update) | async-done | bytes 6291472 | tf_op jit(solution)/shard_map/all_gather | solution.py:43
  98.2 45.1 %all-gather.8.cloned.1.call-done = bf16[2,128,6144]{2,1,0:T(8,128)(2,1)} async-done(((bf16[1,128,6144]{2,1,0:T(8,128)(2,1)}), bf16[2,128,6144]{2,1,0:T(8,128)(2,1)}) %all-gather.8.cloned.1.call-update) | async-done | bytes 3145744 | tf_op jit(solution)/shard_map/all_gather | solution.py:31
  145.4 360.6 %while.14 = (s32[]{:T(128)}, f32[8,8,256,512]{3,2,1,0:T(8,128)}, s32[8]{0:T(128)S(1)}, s32[]{:T(128)}, bf16[256,6400]{1,0:T(8,128)(2,1)S(1)}, /*index=5*/bf16[51...) while((s32[]{:T(128)}, f32[8,8,256,512]{3,2,1,0:T(8,128)}, ...), condition=%wide.region_1.2_spmd, body=%wide.region_0.1_spmd.sunk | while | flops 12884901888 | bytes 85984392 | solution.py:26
  146.7 2.8 bitcast_dynamic-update-slice_fusion.18
  149.5 2.9 bitcast_dynamic-update-slice_fusion.19
  152.4 2.9 bitcast_dynamic-update-slice_fusion.20
  155.3 2.8 bitcast_dynamic-update-slice_fusion.21
  160.9 2.8 bitcast_dynamic-update-slice_fusion.23
  163.8 2.8 bitcast_dynamic-update-slice_fusion.24
  166.6 2.8 bitcast_dynamic-update-slice_fusion.25
  169.4 21.0 %bitcast_dynamic-update-slice_fusion.26 = f32[8,8,256,512]{3,2,1,0:T(8,128)} fusion(f32[8,8,256,512]{3,2,1,0:T(8,128)} %get-tuple-element.216, s32[]{:T(128)} %get-tuple-element.215, bf16[8,256,6144]{2,1,0:T(8,128)(2,1)} %bitcast_dynamic-update-slice_fusion.25, bf16[512,6144]{1,0:T(8,128)(2,1)} %get-tuple-element.245), kind=kOutput, calls=%fused_computation.2.clone.1 | convolution fusion | flops 12884901888 | bytes 35652096 | tf_op jit(solution)/shard_map/while/body/eval_jaxpr/kit,jt->kij/dot_general | solution.py:24
  191.8 2.8 bitcast_dynamic-update-slice_fusion.18
  194.6 2.9 bitcast_dynamic-update-slice_fusion.19
  197.5 2.9 bitcast_dynamic-update-slice_fusion.20
  200.4 2.8 bitcast_dynamic-update-slice_fusion.21
  206.0 2.8 bitcast_dynamic-update-slice_fusion.23
  208.8 2.8 bitcast_dynamic-update-slice_fusion.24
  211.7 2.8 bitcast_dynamic-update-slice_fusion.25
  214.5 21.1 %bitcast_dynamic-update-slice_fusion.26 = f32[8,8,256,512]{3,2,1,0:T(8,128)} fusion(f32[8,8,256,512]{3,2,1,0:T(8,128)} %get-tuple-element.216, s32[]{:T(128)} %get-tuple-element.215, bf16[8,256,6144]{2,1,0:T(8,128)(2,1)} %bitcast_dynamic-update-slice_fusion.25, bf16[512,6144]{1,0:T(8,128)(2,1)} %get-tuple-element.245), kind=kOutput, calls=%fused_computation.2.clone.1 | convolution fusion | flops 12884901888 | bytes 35652096 | tf_op jit(solution)/shard_map/while/body/eval_jaxpr/kit,jt->kij/dot_general | solution.py:24
  236.8 2.8 bitcast_dynamic-update-slice_fusion.18
  239.7 2.9 bitcast_dynamic-update-slice_fusion.19
  242.6 2.9 bitcast_dynamic-update-slice_fusion.20
  245.4 2.8 bitcast_dynamic-update-slice_fusion.21
  251.1 2.8 bitcast_dynamic-update-slice_fusion.23
  256.8 2.8 bitcast_dynamic-update-slice_fusion.25
  259.6 21.1 %bitcast_dynamic-update-slice_fusion.26 = f32[8,8,256,512]{3,2,1,0:T(8,128)} fusion(f32[8,8,256,512]{3,2,1,0:T(8,128)} %get-tuple-element.216, s32[]{:T(128)} %get-tuple-element.215, bf16[8,256,6144]{2,1,0:T(8,128)(2,1)} %bitcast_dynamic-update-slice_fusion.25, bf16[512,6144]{1,0:T(8,128)(2,1)} %get-tuple-element.245), kind=kOutput, calls=%fused_computation.2.clone.1 | convolution fusion | flops 12884901888 | bytes 35652096 | tf_op jit(solution)/shard_map/while/body/eval_jaxpr/kit,jt->kij/dot_general | solution.py:24
  281.9 2.8 bitcast_dynamic-update-slice_fusion.18
  284.8 2.9 bitcast_dynamic-update-slice_fusion.19
  287.6 2.9 bitcast_dynamic-update-slice_fusion.20
  290.5 2.8 bitcast_dynamic-update-slice_fusion.21
  296.2 2.8 bitcast_dynamic-update-slice_fusion.23
  301.8 2.8 bitcast_dynamic-update-slice_fusion.25
  304.7 21.1 %bitcast_dynamic-update-slice_fusion.26 = f32[8,8,256,512]{3,2,1,0:T(8,128)} fusion(f32[8,8,256,512]{3,2,1,0:T(8,128)} %get-tuple-element.216, s32[]{:T(128)} %get-tuple-element.215, bf16[8,256,6144]{2,1,0:T(8,128)(2,1)} %bitcast_dynamic-update-slice_fusion.25, bf16[512,6144]{1,0:T(8,128)(2,1)} %get-tuple-element.245), kind=kOutput, calls=%fused_computation.2.clone.1 | convolution fusion | flops 12884901888 | bytes 35652096 | tf_op jit(solution)/shard_map/while/body/eval_jaxpr/kit,jt->kij/dot_general | solution.py:24
  327.0 2.8 bitcast_dynamic-update-slice_fusion.18
  329.8 2.9 bitcast_dynamic-update-slice_fusion.19
  332.7 2.9 bitcast_dynamic-update-slice_fusion.20
  335.6 2.8 bitcast_dynamic-update-slice_fusion.21
  341.2 2.8 bitcast_dynamic-update-slice_fusion.23
  346.9 2.8 bitcast_dynamic-update-slice_fusion.25
  349.7 21.1 %bitcast_dynamic-update-slice_fusion.26 = f32[8,8,256,512]{3,2,1,0:T(8,128)} fusion(f32[8,8,256,512]{3,2,1,0:T(8,128)} %get-tuple-element.216, s32[]{:T(128)} %get-tuple-element.215, bf16[8,256,6144]{2,1,0:T(8,128)(2,1)} %bitcast_dynamic-update-slice_fusion.25, bf16[512,6144]{1,0:T(8,128)(2,1)} %get-tuple-element.245), kind=kOutput, calls=%fused_computation.2.clone.1 | convolution fusion | flops 12884901888 | bytes 35652096 | tf_op jit(solution)/shard_map/while/body/eval_jaxpr/kit,jt->kij/dot_general | solution.py:24
  372.1 2.8 bitcast_dynamic-update-slice_fusion.18
  374.9 2.9 bitcast_dynamic-update-slice_fusion.19
  377.8 2.9 bitcast_dynamic-update-slice_fusion.20
  380.7 2.8 bitcast_dynamic-update-slice_fusion.21
  386.3 2.8 bitcast_dynamic-update-slice_fusion.23
  392.0 2.8 bitcast_dynamic-update-slice_fusion.25
  394.8 21.1 %bitcast_dynamic-update-slice_fusion.26 = f32[8,8,256,512]{3,2,1,0:T(8,128)} fusion(f32[8,8,256,512]{3,2,1,0:T(8,128)} %get-tuple-element.216, s32[]{:T(128)} %get-tuple-element.215, bf16[8,256,6144]{2,1,0:T(8,128)(2,1)} %bitcast_dynamic-update-slice_fusion.25, bf16[512,6144]{1,0:T(8,128)(2,1)} %get-tuple-element.245), kind=kOutput, calls=%fused_computation.2.clone.1 | convolution fusion | flops 12884901888 | bytes 35652096 | tf_op jit(solution)/shard_map/while/body/eval_jaxpr/kit,jt->kij/dot_general | solution.py:24
  417.2 2.8 bitcast_dynamic-update-slice_fusion.18
  420.0 2.9 bitcast_dynamic-update-slice_fusion.19
  422.9 2.9 bitcast_dynamic-update-slice_fusion.20
  425.7 2.8 bitcast_dynamic-update-slice_fusion.21
  431.4 2.8 bitcast_dynamic-update-slice_fusion.23
  437.1 2.8 bitcast_dynamic-update-slice_fusion.25
  439.9 21.1 %bitcast_dynamic-update-slice_fusion.26 = f32[8,8,256,512]{3,2,1,0:T(8,128)} fusion(f32[8,8,256,512]{3,2,1,0:T(8,128)} %get-tuple-element.216, s32[]{:T(128)} %get-tuple-element.215, bf16[8,256,6144]{2,1,0:T(8,128)(2,1)} %bitcast_dynamic-update-slice_fusion.25, bf16[512,6144]{1,0:T(8,128)(2,1)} %get-tuple-element.245), kind=kOutput, calls=%fused_computation.2.clone.1 | convolution fusion | flops 12884901888 | bytes 35652096 | tf_op jit(solution)/shard_map/while/body/eval_jaxpr/kit,jt->kij/dot_general | solution.py:24
  462.2 2.8 bitcast_dynamic-update-slice_fusion.18
  465.1 2.9 bitcast_dynamic-update-slice_fusion.19
  467.9 2.9 bitcast_dynamic-update-slice_fusion.20
  470.8 2.8 bitcast_dynamic-update-slice_fusion.21
  476.5 2.8 bitcast_dynamic-update-slice_fusion.23
  482.1 2.8 bitcast_dynamic-update-slice_fusion.25
  485.0 21.1 %bitcast_dynamic-update-slice_fusion.26 = f32[8,8,256,512]{3,2,1,0:T(8,128)} fusion(f32[8,8,256,512]{3,2,1,0:T(8,128)} %get-tuple-element.216, s32[]{:T(128)} %get-tuple-element.215, bf16[8,256,6144]{2,1,0:T(8,128)(2,1)} %bitcast_dynamic-update-slice_fusion.25, bf16[512,6144]{1,0:T(8,128)(2,1)} %get-tuple-element.245), kind=kOutput, calls=%fused_computation.2.clone.1 | convolution fusion | flops 12884901888 | bytes 35652096 | tf_op jit(solution)/shard_map/while/body/eval_jaxpr/kit,jt->kij/dot_general | solution.py:24
  506.0 23.9 %broadcast_multiply_fusion = f32[8,8,256,512]{3,2,1,0:T(8,128)} fusion(f32[8,8,256,512]{3,2,1,0:T(8,128)} %get-tuple-element.140), kind=kLoop, calls=%fused_computation.11 | loop fusion | flops 8388608 | bytes 67108864 | tf_op jit(solution)/shard_map/mul | solution.py:55
  530.0 48.4 %mul.39 = f32[64,2,128,1,512]{4,3,2,1,0:T(1,128)} reshape(f32[8,8,256,512]{3,2,1,0:T(8,128)} %broadcast_multiply_fusion) | data formatting | bytes 67108864 | tf_op jit(solution)/shard_map/mul | solution.py:55
  (32 shorter events, 50.2 us)
Async XLA Ops:
  6.5 42.1 %all-gather.4.cloned.1.call-start = ((), (), s32[]{:S(2)}) async-start(), calls=%async_computation | async-start | bytes 1966080 | tf_op jit(solution)/shard_map/all_gather | solution.py:42
  7.3 88.2 %all-gather.6.cloned.1.call-start = ((), (), s32[]{:S(2)}) async-start(), calls=%async_computation.1 | async-start | bytes 7864320 | tf_op jit(solution)/shard_map/all_gather | solution.py:43
  48.7 94.6 %all-gather.8.cloned.1.call-start = ((), (), s32[]{:S(2)}) async-start(), calls=%async_computation.2 | async-start | bytes 4718592 | tf_op jit(solution)/shard_map/all_gather | solution.py:31
Sparse Core Ops, SparseCore 0:
  8.9 39.7 all-gather.3
  50.2 45.2 all-gather.5
  98.3 44.9 all-gather.7
where the time goes:
time: 586 us; the launch traced here: 585 us
  local copies, waits for them, and re-layouts  240 us (41%)
  matrix products  168 us (29%)
  waiting for transfers between devices  134 us (23%)
  other arithmetic  23.9 us (4%)
  between operations  13.1 us (2%)
    dot_general x8, matrix products, one_group(): jnp.einsum('kit,jt->kij', stacked, flat_cols, preferred_element_type=jnp....  168 us
    while x56, local copies, waits for them, and re-layouts  159 us
    mul x1, local copies, waits for them, and re-layouts, per_device(): return accumulated_sum * factor  48.4 us
    all_gather x1, waiting for transfers between devices, per_device(): columns = lax.all_gather(col_tiles, 'tm', axis=2, tiled=True)  46.7 us
    all_gather x1, waiting for transfers between devices, collect_rows(): return lax.all_gather(own_window, 'antb', axis=0, tiled=True)  45.1 us
    all_gather x1, waiting for transfers between devices, per_device(): col_tiles = lax.all_gather(samples, 'anta', axis=1, tiled=True)  41.4 us
    mul x1, other arithmetic, per_device(): return accumulated_sum * factor  23.9 us
    another operation x8, local copies, waits for them, and re-layouts, one_group(): stacked = jnp.stack(pieces, 0)  22.7 us
  transfers between devices with their start and end apart: 3, of which 3 were waited for; matrix products, arithmetic and copies ran while one was open for 0% of the time, Pallas kernels for 0%

commit v1 on v0

v1 whole, which is shorter than its diff:
```python
import math

import jax
import jax.numpy as jnp
from jax import lax
from jax.experimental import pallas as pl
from jax.experimental.pallas import tpu as pltpu
from jax.sharding import PartitionSpec as P

POLARISATION_NUM = 2
LAG_TOTAL = 256
FINE = 16
PER_STEP = 2
LANES = 128
STRIP = 16


def lag_kernel(row_ref, col_ref, *refs, coarse, factor, lag_portion, parts, part_of):
    *prev, out_ref, state_ref, shifted_ref, wide_ref = refs
    row_count, window = row_ref.shape
    col_count = col_ref.shape[1]
    part_chunks = col_count // LANES
    chunks = part_chunks * parts
    lag_start = lax.axis_index("tm") * lag_portion
    first_chunk = part_of() * part_chunks

    @pl.when(pl.program_id(0) == 0)
    def _():
        state_ref[:, window:] = jnp.zeros((row_count, LANES), jnp.bfloat16)
        wide_ref[window:, :] = jnp.zeros((LAG_TOTAL, col_count), jnp.bfloat16)

        def fill_rows(index, carry):
            at = pl.multiple_of(index * STRIP, STRIP)
            state_ref[pl.ds(at, STRIP), :window] = row_ref[pl.ds(at, STRIP), :]
            return carry

        def fill_cols(index, carry):
            at = pl.multiple_of(index * LANES, LANES)
            wide_ref[pl.ds(at, LANES), :] = col_ref[pl.ds(at, LANES), :]
            return carry

        lax.fori_loop(0, row_count // STRIP, fill_rows, 0)
        lax.fori_loop(0, window // LANES, fill_cols, 0)

    def shift_strip(index, carry):
        at = pl.multiple_of(index * STRIP, STRIP)
        wide = state_ref[pl.ds(at, STRIP), :].astype(jnp.float32)
        for step in range(PER_STEP):
            to = pl.multiple_of(step * row_count + index * STRIP, STRIP)
            shifted_ref[pl.ds(to, STRIP), :] = wide[:, :window].astype(jnp.bfloat16)
            wide = pltpu.roll(wide, 1, 1)
        state_ref[pl.ds(at, STRIP), :] = wide.astype(jnp.bfloat16)
        return carry

    lax.fori_loop(0, row_count // STRIP, shift_strip, 0)

    def coarse_lag(step, carry):
        start = pl.multiple_of(lag_start + step * FINE, FINE)
        product = jnp.dot(
            shifted_ref[...], wide_ref[pl.ds(start, window), :], preferred_element_type=jnp.float32
        ) * factor
        for fine in range(PER_STEP):
            if prev:
                out_ref[step, fine] = prev[0][step, fine]
            for chunk in range(part_chunks):
                out_ref[step, fine, pl.ds(first_chunk + chunk, row_count, stride=chunks), :] = product[
                    fine * row_count : (fine + 1) * row_count, chunk * LANES : (chunk + 1) * LANES
                ]
        return carry

    lax.fori_loop(0, coarse, coarse_lag, 0)


def lag_products(rows, columns, prev, lag_portion, parts, part_of):
    row_count, window = rows.shape
    col_count = columns.shape[1]
    coarse = lag_portion // FINE
    out_rows = row_count * parts * (col_count // LANES)

    def kernel(*refs):
        lag_kernel(
            *refs, coarse=coarse, factor=1.0 / math.sqrt(window), lag_portion=lag_portion,
            parts=parts, part_of=part_of,
        )

    whole = pl.BlockSpec(memory_space=pltpu.VMEM)
    block = pl.BlockSpec((coarse, PER_STEP, out_rows, LANES), lambda m: (0, m, 0, 0))
    return pl.pallas_call(
        kernel,
        grid=(FINE // PER_STEP,),
        in_specs=[whole, whole] + [block] * len(prev),
        out_specs=block,
        out_shape=jax.ShapeDtypeStruct((coarse, FINE, out_rows, LANES), jnp.float32),
        scratch_shapes=[
            pltpu.VMEM((row_count, window + LANES), jnp.bfloat16),
            pltpu.VMEM((PER_STEP * row_count, window), jnp.bfloat16),
            pltpu.VMEM((window + LAG_TOTAL, col_count), jnp.bfloat16),
        ],
        input_output_aliases={2: 0} if prev else {},
        compiler_params=pltpu.CompilerParams(vmem_limit_bytes=56 * 1024 * 1024),
        name="lag_products",
    )(rows, columns, *prev)


def swap(array, axis, distance, size):
    return lax.ppermute(array, axis, [(i, (i + distance) % size) for i in range(size)])


def per_device(samples):
    own = samples[0]
    own_antennas, block_len = own.shape
    tm_size = lax.axis_size("tm")
    anta_size = lax.axis_size("anta")
    lag_portion = LAG_TOTAL // tm_size
    antenna_total = own_antennas * anta_size
    half = anta_size // 2
    anta_at = lax.axis_index("anta")

    other = swap(own, "antb", 1, POLARISATION_NUM)
    first = lax.axis_index("antb") == 0
    both = jnp.concatenate([jnp.where(first, own, other), jnp.where(first, other, own)], 0)
    rows = lax.all_gather(both, "tm", axis=1, tiled=True)

    turned = own.T
    if half == 2:
        pairs = [(i, i ^ 1) for i in range(anta_size)]
        beside = lax.ppermute(turned, "anta", pairs)
        even = anta_at % 2 == 0
        near = jnp.concatenate([jnp.where(even, turned, beside), jnp.where(even, beside, turned)], 1)
    else:
        groups = [list(range(half)), list(range(half, anta_size))]
        near = lax.all_gather(turned, "anta", axis=1, tiled=True, axis_index_groups=groups)
    far = swap(near, "anta", half, anta_size)
    near_columns = lax.all_gather(near, "tm", axis=0, tiled=True)
    far_columns = lax.all_gather(far, "tm", axis=0, tiled=True)

    def near_part():
        return lax.axis_index("anta") // half

    def far_part():
        return 1 - lax.axis_index("anta") // half

    out = lag_products(rows, near_columns, (), lag_portion, 2, near_part)
    out = lag_products(rows, far_columns, (out,), lag_portion, 2, far_part)
    return out.reshape(lag_portion, POLARISATION_NUM, own_antennas, 1, antenna_total)


def solution(mesh):
    return jax.shard_map(
        per_device,
        mesh=mesh,
        in_specs=(P("antb", "anta", "tm"),),
        out_specs=P("tm", None, "anta", "antb", None),
        check_vma=False,
    )
```

time: 586 us -> 281 us (0.48)
  local copies, waits for them, and re-layouts: 240 us -> 6.75 us
  Pallas kernels: 0 us -> 193 us
  matrix products: 168 us -> 0 us
  waiting for transfers between devices: 134 us -> 58.1 us
  other arithmetic: 23.9 us -> 2.12 us
  starting transfers between devices: 0.08 us -> 7.6 us
    pallas_call x0 -> x2, Pallas kernels: none -> 193 us  [lag_products(): pl.pallas_call(kernel, grid=(FINE // PER_STEP,), in_specs=[whole, whole]...]
    dot_general x8 -> x0, matrix products: 168 us -> none  [one_group(): jnp.einsum('kit,jt->kij', stacked, flat_cols, preferred_element_type=jnp....]
    while x56 -> x0, local copies, waits for them, and re-layouts: 159 us -> none
    all_gather x3, waiting for transfers between devices: 133 us -> 7.2 us  [the longest x1 7.18 us: per_device(): near_columns = lax.all_gather(near, 'tm', axis=0, tiled=True)]
    ppermute x0 -> x3, waiting for transfers between devices: none -> 50.9 us  [the longest x2 42.4 us: swap(): lax.ppermute(array, axis, [(i, (i + distance) % size) for i in range(size)])]
    mul x1 -> x0, local copies, waits for them, and re-layouts: 48.4 us -> none  [per_device(): return accumulated_sum * factor]
    mul x1 -> x0, other arithmetic: 23.9 us -> none  [per_device(): return accumulated_sum * factor]
    another operation x8 -> x0, local copies, waits for them, and re-layouts: 22.7 us -> none  [one_group(): stacked = jnp.stack(pieces, 0)]
  transfers between devices with their start and end apart: 3 -> 6, of which waited for: 3 -> 4; matrix products, arithmetic and copies ran while one was open for 0% -> 2% of each run, Pallas kernels for 0% -> 34%
where the time goes in v1:
time: 281 us
  Pallas kernels  193 us (69%)
  waiting for transfers between devices  58.1 us (21%)
  between operations  13.1 us (5%)
  starting transfers between devices  7.6 us (3%)
  local copies, waits for them, and re-layouts  6.75 us (2%)
    pallas_call x2, Pallas kernels, lag_products(): pl.pallas_call(kernel, grid=(FINE // PER_STEP,), in_specs=[whole, whole]...  193 us
    ppermute x2, waiting for transfers between devices, swap(): lax.ppermute(array, axis, [(i, (i + distance) % size) for i in range(size)])  42.4 us
    ppermute x1, waiting for transfers between devices, per_device(): beside = lax.ppermute(turned, 'anta', pairs)  8.48 us
    all_gather x1, waiting for transfers between devices, per_device(): near_columns = lax.all_gather(near, 'tm', axis=0, tiled=True)  7.18 us
    ppermute x2, starting transfers between devices, swap(): lax.ppermute(array, axis, [(i, (i + distance) % size) for i in range(size)])  5.66 us
  transfers between devices with their start and end apart: 6, of which 4 were waited for; matrix products, arithmetic and copies ran while one was open for 2% of the time, Pallas kernels for 34%

profile of v1, /device:TPU:0, one launch (start us, length us, event | category | flops | bytes accessed | tf_op | source)
XLA Modules:
  0.0 281.0 jit_solution(11470094619737863548)
XLA Ops:
  6.5 0.0 all-gather.4.cloned.1.call-start
  6.5 1.2 copy.3
  7.8 3.1 %collective-permute-start = (bf16[128,1536]{0,1:T(8,128)(2,1)S(1)}, bf16[128,1536]{0,1:T(8,128)(2,1)S(1)}, u32[]{:S(2)}, u32[]{:S(2)}) collective-permute-start(bf16[128,1536]{0,1:T(8,128)(2,1)S(1)} %bitcast.8), channel_id=1, source_target_pairs={{0,1},{1,0},{2,3},{3,2},{4,5},{5,4},{6,7},{7,6},{8,9},{9,8},{10,11... | collective-permute-start | bytes 1179656 | tf_op jit(solution)/shard_map/ppermute | solution.py:106
  10.8 9.1 %collective-permute-done = bf16[128,1536]{0,1:T(8,128)(2,1)S(1)} collective-permute-done((bf16[128,1536]{0,1:T(8,128)(2,1)S(1)}, bf16[128,1536]{0,1:T(8,128)(2,1)S(1)}, u32[]{:S(2)}, u32[]{:S(2)}) %collective-permute-start) | collective-permute-done | bytes 393248 | tf_op jit(solution)/shard_map/ppermute | solution.py:106
  19.9 0.1 broadcast_select_fusion.3
  20.0 1.0 pad_maximum_fusion
  21.0 0.0 all-gather.4.cloned.1.call-update
  21.0 0.0 all-gather.8.cloned.1.call-start
  21.0 1.9 collective-permute-start.1
  22.9 8.5 %collective-permute-done.1 = bf16[1536,128]{1,0:T(8,128)(2,1)S(1)} collective-permute-done((bf16[1536,128]{1,0:T(8,128)(2,1)S(1)}, bf16[1536,128]{1,0:T(8,128)(2,1)S(1)}, u32[]{:S(2)}, u32[]{:S(2)}) %collective-permute-start.1) | collective-permute-done | bytes 393248 | tf_op jit(solution)/shard_map/ppermute | solution.py:127
  31.4 0.1 broadcast_select_fusion.1
  31.4 1.0 pad_maximum_fusion.1
  32.5 0.0 all-gather.8.cloned.1.call-update
  32.5 0.0 all-gather.6.cloned.1.call-start
  32.6 2.6 collective-permute-start.2
  35.2 33.3 %collective-permute-done.2 = bf16[1536,256]{1,0:T(8,128)(2,1)S(1)} collective-permute-done((bf16[1536,256]{1,0:T(8,128)(2,1)}, bf16[1536,256]{1,0:T(8,128)(2,1)S(1)}, u32[]{:S(2)}, u32[]{:S(2)}) %collective-permute-start.2) | collective-permute-done | bytes 786464 | tf_op jit(solution)/shard_map/ppermute | solution.py:106
  68.4 0.0 copy-start
  68.4 0.9 copy-done
  69.3 0.0 all-gather.6.cloned.1.call-update
  69.4 0.0 all-gather.4.cloned.1.call-done
  69.4 4.7 %copy.5.refs_0_ = bf16[256,6144]{1,0:T(8,128)(2,1)} copy(bf16[256,6144]{0,1:T(8,128)(2,1)} %all-gather.4.cloned.1.call-done) | data formatting | bytes 6291456 | tf_op jit(solution)/shard_map/all_gather | solution.py:122
  74.0 7.2 %all-gather.8.cloned.1.call-done.refs_1_ = bf16[6144,256]{1,0:T(8,128)(2,1)} async-done(((bf16[1536,256]{1,0:T(8,128)(2,1)}), bf16[6144,256]{1,0:T(8,128)(2,1)}) %all-gather.8.cloned.1.call-update) | async-done | bytes 3145744 | tf_op jit(solution)/shard_map/all_gather | solution.py:134
  81.2 95.8 %lag_products.2.refs_2_ = f32[4,16,1024,128]{3,2,1,0:T(8,128)} custom-call(bf16[256,6144]{1,0:T(8,128)(2,1)} %copy.5.refs_0_, bf16[6144,256]{1,0:T(8,128)(2,1)} %all-gather.8.cloned.1.call-done.refs_1_), custom_call_target="tpu_custom_call" | custom-call | tf_op jit(solution)/shard_map/lag_products/pallas_call | solution.py:88
  177.0 0.0 all-gather.6.cloned.1.call-done.refs_1_
  177.0 97.5 %lag_products.3 = f32[4,16,1024,128]{3,2,1,0:T(8,128)} custom-call(bf16[256,6144]{1,0:T(8,128)(2,1)} %copy.5.refs_0_, bf16[6144,256]{1,0:T(8,128)(2,1)} %all-gather.6.cloned.1.call-done.refs_1_, f32[4,16,1024,128]{3,2,1,0:T(8,128)} %lag_products.2.refs_2_), custom_call_target="tpu_custom_call", output_to_operand_aliasing={{}: (2, {})} | custom-call | tf_op jit(solution)/shard_map/lag_products/pallas_call | solution.py:88
Async XLA Ops:
  6.5 62.8 %all-gather.4.cloned.1.call-start = ((), (), s32[]{:S(2)}) async-start(), calls=%async_computation | async-start | bytes 3932160 | tf_op jit(solution)/shard_map/all_gather | solution.py:122
  7.8 12.2 %collective-permute-start = (bf16[128,1536]{0,1:T(8,128)(2,1)S(1)}, bf16[128,1536]{0,1:T(8,128)(2,1)S(1)}, u32[]{:S(2)}, u32[]{:S(2)}) collective-permute-start(bf16[128,1536]{0,1:T(8,128)(2,1)S(1)} %bitcast.8), channel_id=1, source_target_pairs={{0,1},{1,0},{2,3},{3,2},{4,5},{5,4},{6,7},{7,6},{8,9},{9,8},{10,11... | collective-permute-start | bytes 1179656 | tf_op jit(solution)/shard_map/ppermute | solution.py:106
  21.0 60.2 %all-gather.8.cloned.1.call-start = ((), (), s32[]{:S(2)}) async-start(), calls=%async_computation.2 | async-start | bytes 3932160 | tf_op jit(solution)/shard_map/all_gather | solution.py:134
  21.0 10.3 %collective-permute-start.1 = (bf16[1536,128]{1,0:T(8,128)(2,1)S(1)}, bf16[1536,128]{1,0:T(8,128)(2,1)S(1)}, u32[]{:S(2)}, u32[]{:S(2)}) collective-permute-start(bf16[1536,128]{1,0:T(8,128)(2,1)S(1)} %bitcast.9), channel_id=1, source_target_pairs={{0,2},{2,0},{4,6},{6,4},{1,3},{3,1},{5,7},{7,5},{8,10},{10,8},{12,... | collective-permute-start | bytes 1179656 | tf_op jit(solution)/shard_map/ppermute | solution.py:127
  32.5 144.5 %all-gather.6.cloned.1.call-start = ((), (), s32[]{:S(2)}) async-start(), calls=%async_computation.1 | async-start | bytes 3932160 | tf_op jit(solution)/shard_map/all_gather | solution.py:135
  32.6 35.9 %collective-permute-start.2 = (bf16[1536,256]{1,0:T(8,128)(2,1)}, bf16[1536,256]{1,0:T(8,128)(2,1)S(1)}, u32[]{:S(2)}, u32[]{:S(2)}) collective-permute-start(bf16[1536,256]{1,0:T(8,128)(2,1)} %pad_maximum_fusion.1), channel_id=1, source_target_pairs={{0,4},{2,6},{4,0},{6,2},{1,5},{3,7},{5,1},{7,3},{8,12},{10,14},{12... | collective-permute-start | bytes 2359304 | tf_op jit(solution)/shard_map/ppermute | solution.py:106
  68.4 0.9 copy-start
Sparse Core Ops, SparseCore 0:
  21.1 29.9 all-gather.3
  52.7 28.4 all-gather.7
  82.8 28.5 all-gather.5

commit v2 on v1

--- a/solution.py
+++ b/solution.py
@@ -15,9 +15,34 @@
 STRIP = 16
 
 
-def lag_kernel(row_ref, col_ref, *refs, coarse, factor, lag_portion, parts, part_of):
-    *prev, out_ref, state_ref, shifted_ref, wide_ref = refs
-    row_count, window = row_ref.shape
+def shift_kernel(row_ref, out_ref):
+    window = row_ref.shape[1]
+    wide = row_ref[...].astype(jnp.float32)
+    wide = jnp.concatenate([wide, jnp.zeros((STRIP, LANES), jnp.float32)], 1)
+    for fine in range(FINE):
+        out_ref[fine] = wide[:, :window].astype(jnp.bfloat16)
+        if fine + 1 < FINE:
+            wide = pltpu.roll(wide, 1, 1)
+
+
+def shifted_rows(rows):
+    row_count, window = rows.shape
+    out = pl.pallas_call(
+        shift_kernel,
+        grid=(row_count // STRIP,),
+        in_specs=[pl.BlockSpec((STRIP, window), lambda i: (i, 0))],
+        out_specs=pl.BlockSpec((FINE, STRIP, window), lambda i: (0, i, 0)),
+        out_shape=jax.ShapeDtypeStruct((FINE, row_count, window), jnp.bfloat16),
+        compiler_params=pltpu.CompilerParams(vmem_limit_bytes=32 * 1024 * 1024),
+        name="shifted_rows",
+    )(rows)
+    return out.reshape(FINE * row_count, window)
+
+
+def lag_kernel(shifted_ref, col_ref, *refs, coarse, factor, lag_portion, parts, part_of):
+    *prev, out_ref, wide_ref = refs
+    stacked, window = shifted_ref.shape
+    row_count = stacked // PER_STEP
     col_count = col_ref.shape[1]
     part_chunks = col_count // LANES
     chunks = part_chunks * parts
@@ -26,33 +51,14 @@
 
     @pl.when(pl.program_id(0) == 0)
     def _():
-        state_ref[:, window:] = jnp.zeros((row_count, LANES), jnp.bfloat16)
         wide_ref[window:, :] = jnp.zeros((LAG_TOTAL, col_count), jnp.bfloat16)
-
-        def fill_rows(index, carry):
-            at = pl.multiple_of(index * STRIP, STRIP)
-            state_ref[pl.ds(at, STRIP), :window] = row_ref[pl.ds(at, STRIP), :]
-            return carry
 
         def fill_cols(index, carry):
             at = pl.multiple_of(index * LANES, LANES)
             wide_ref[pl.ds(at, LANES), :] = col_ref[pl.ds(at, LANES), :]
             return carry
 
-        lax.fori_loop(0, row_count // STRIP, fill_rows, 0)
         lax.fori_loop(0, window // LANES, fill_cols, 0)
-
-    def shift_strip(index, carry):
-        at = pl.multiple_of(index * STRIP, STRIP)
-        wide = state_ref[pl.ds(at, STRIP), :].astype(jnp.float32)
-        for step in range(PER_STEP):
-            to = pl.multiple_of(step * row_count + index * STRIP, STRIP)
-            shifted_ref[pl.ds(to, STRIP), :] = wide[:, :window].astype(jnp.bfloat16)
-            wide = pltpu.roll(wide, 1, 1)
-        state_ref[pl.ds(at, STRIP), :] = wide.astype(jnp.bfloat16)
-        return carry
-
-    lax.fori_loop(0, row_count // STRIP, shift_strip, 0)
 
     def coarse_lag(step, carry):
         start = pl.multiple_of(lag_start + step * FINE, FINE)
@@ -71,8 +77,8 @@
     lax.fori_loop(0, coarse, coarse_lag, 0)
 
 
-def lag_products(rows, columns, prev, lag_portion, parts, part_of):
-    row_count, window = rows.shape
+def lag_products(shifted, columns, prev, lag_portion, parts, part_of):
+    row_count, window = shifted.shape[0] // FINE, shifted.shape[1]
     col_count = columns.shape[1]
     coarse = lag_portion // FINE
     out_rows = row_count * parts * (col_count // LANES)
@@ -88,18 +94,16 @@
     return pl.pallas_call(
         kernel,
         grid=(FINE // PER_STEP,),
-        in_specs=[whole, whole] + [block] * len(prev),
+        in_specs=[pl.BlockSpec((PER_STEP * row_count, window), lambda m: (m, 0)), whole] + [block] * len(prev),
         out_specs=block,
         out_shape=jax.ShapeDtypeStruct((coarse, FINE, out_rows, LANES), jnp.float32),
         scratch_shapes=[
-            pltpu.VMEM((row_count, window + LANES), jnp.bfloat16),
-            pltpu.VMEM((PER_STEP * row_count, window), jnp.bfloat16),
             pltpu.VMEM((window + LAG_TOTAL, col_count), jnp.bfloat16),
         ],
         input_output_aliases={2: 0} if prev else {},
         compiler_params=pltpu.CompilerParams(vmem_limit_bytes=56 * 1024 * 1024),
         name="lag_products",
-    )(rows, columns, *prev)
+    )(shifted, columns, *prev)
 
 
 def swap(array, axis, distance, size):
@@ -119,9 +123,9 @@
     other = swap(own, "antb", 1, POLARISATION_NUM)
     first = lax.axis_index("antb") == 0
     both = jnp.concatenate([jnp.where(first, own, other), jnp.where(first, other, own)], 0)
+
+    both, turned = lax.optimization_barrier((both, own.T))
     rows = lax.all_gather(both, "tm", axis=1, tiled=True)
-
-    turned = own.T
     if half == 2:
         pairs = [(i, i ^ 1) for i in range(anta_size)]
         beside = lax.ppermute(turned, "anta", pairs)
@@ -130,9 +134,8 @@
     else:
         groups = [list(range(half)), list(range(half, anta_size))]
         near = lax.all_gather(turned, "anta", axis=1, tiled=True, axis_index_groups=groups)
-    far = swap(near, "anta", half, anta_size)
     near_columns = lax.all_gather(near, "tm", axis=0, tiled=True)
-    far_columns = lax.all_gather(far, "tm", axis=0, tiled=True)
+    far_columns = swap(near_columns, "anta", half, anta_size)
 
     def near_part():
         return lax.axis_index("anta") // half
@@ -140,8 +143,9 @@
     def far_part():
         return 1 - lax.axis_index("anta") // half
 
-    out = lag_products(rows, near_columns, (), lag_portion, 2, near_part)
-    out = lag_products(rows, far_columns, (out,), lag_portion, 2, far_part)
+    shifted = shifted_rows(rows)
+    out = lag_products(shifted, near_columns, (), lag_portion, 2, near_part)
+    out = lag_products(shifted, far_columns, (out,), lag_portion, 2, far_part)
     return out.reshape(lag_portion, POLARISATION_NUM, own_antennas, 1, antenna_total)
 
 

time: 281 us -> 274 us (0.975)
  Pallas kernels: 193 us -> 161 us
  waiting for transfers between devices: 58.1 us -> 85.3 us
    pallas_call x2 -> x3, Pallas kernels: 193 us -> 161 us  [the longest x2 130 us: lag_products(): pl.pallas_call(kernel, grid=(FINE // PER_STEP,), in_specs=[pl.BlockSpec((...]
    all_gather x1, waiting for transfers between devices: 0.02 us -> 27.7 us  [per_device(): rows = lax.all_gather(both, 'tm', axis=1, tiled=True)]
    ppermute x2, waiting for transfers between devices: 42.4 us -> 19.3 us  [swap(): lax.ppermute(array, axis, [(i, (i + distance) % size) for i in range(size)])]
    all_gather x1, waiting for transfers between devices: 7.18 us -> 29.1 us  [per_device(): near_columns = lax.all_gather(near, 'tm', axis=0, tiled=True)]
  transfers between devices with their start and end apart: 6 -> 5, of which waited for: 4 -> 5; matrix products, arithmetic and copies ran while one was open for 2% -> 1% of each run, Pallas kernels for 34% -> 35%
where the time goes in v2:
time: 274 us
  Pallas kernels  161 us (59%)
  waiting for transfers between devices  85.3 us (31%)
  between operations  13.4 us (5%)
  starting transfers between devices  7.31 us (3%)
  local copies, waits for them, and re-layouts  4.39 us (2%)
    pallas_call x2, Pallas kernels, lag_products(): pl.pallas_call(kernel, grid=(FINE // PER_STEP,), in_specs=[pl.BlockSpec((...  130 us
    pallas_call x1, Pallas kernels, shifted_rows(): pl.pallas_call(shift_kernel, grid=(row_count // STRIP,), in_specs=[pl.Blo...  31 us
    all_gather x1, waiting for transfers between devices, per_device(): near_columns = lax.all_gather(near, 'tm', axis=0, tiled=True)  29.1 us
    all_gather x1, waiting for transfers between devices, per_device(): rows = lax.all_gather(both, 'tm', axis=1, tiled=True)  27.7 us
    ppermute x2, waiting for transfers between devices, swap(): lax.ppermute(array, axis, [(i, (i + distance) % size) for i in range(size)])  19.3 us
    ppermute x1, waiting for transfers between devices, per_device(): beside = lax.ppermute(turned, 'anta', pairs)  8.48 us
  transfers between devices with their start and end apart: 5, of which 5 were waited for; matrix products, arithmetic and copies ran while one was open for 1% of the time, Pallas kernels for 35%

profile of v2, /device:TPU:0, one launch (start us, length us, event | category | flops | bytes accessed | tf_op | source)
XLA Modules:
  0.0 273.9 jit_solution(10048159792433179110)
XLA Ops:
  6.5 0.0 all-gather.5.cloned.1.call-start
  6.5 1.2 copy.3
  7.8 3.1 %collective-permute-start = (bf16[128,1536]{0,1:T(8,128)(2,1)S(1)}, bf16[128,1536]{0,1:T(8,128)(2,1)S(1)}, u32[]{:S(2)}, u32[]{:S(2)}) collective-permute-start(bf16[128,1536]{0,1:T(8,128)(2,1)S(1)} %bitcast.9), channel_id=1, source_target_pairs={{0,1},{1,0},{2,3},{3,2},{4,5},{5,4},{6,7},{7,6},{8,9},{9,8},{10,11... | collective-permute-start | bytes 1179656 | tf_op jit(solution)/shard_map/ppermute | solution.py:110
  10.8 9.1 %collective-permute-done = bf16[128,1536]{0,1:T(8,128)(2,1)S(1)} collective-permute-done((bf16[128,1536]{0,1:T(8,128)(2,1)S(1)}, bf16[128,1536]{0,1:T(8,128)(2,1)S(1)}, u32[]{:S(2)}, u32[]{:S(2)}) %collective-permute-start) | collective-permute-done | bytes 393248 | tf_op jit(solution)/shard_map/ppermute | solution.py:110
  19.9 0.1 broadcast_select_fusion.3
  20.0 1.0 pad_maximum_fusion
  21.0 1.8 collective-permute-start.1
  22.8 8.5 %collective-permute-done.1 = bf16[1536,128]{1,0:T(8,128)(2,1)S(1)} collective-permute-done((bf16[1536,128]{1,0:T(8,128)(2,1)S(1)}, bf16[1536,128]{1,0:T(8,128)(2,1)S(1)}, u32[]{:S(2)}, u32[]{:S(2)}) %collective-permute-start.1) | collective-permute-done | bytes 393248 | tf_op jit(solution)/shard_map/ppermute | solution.py:131
  31.2 0.1 broadcast_select_fusion.1
  31.3 1.0 pad_maximum_fusion.1
  32.3 0.0 all-gather.5.cloned.1.call-update
  32.3 0.0 all-gather.3.cloned.1.call-start
  32.4 0.7 all-gather.3.cloned.1.call-update
  33.1 29.1 %all-gather.5.cloned.1.call-done.refs_1_ = bf16[6144,256]{1,0:T(8,128)(2,1)} async-done(((bf16[1536,256]{1,0:T(8,128)(2,1)}), bf16[6144,256]{1,0:T(8,128)(2,1)}) %all-gather.5.cloned.1.call-update) | async-done | bytes 3145744 | tf_op jit(solution)/shard_map/all_gather | solution.py:137
  62.2 2.4 collective-permute-start.2
  64.6 27.7 %all-gather.3.cloned.1.call-done = bf16[256,6144]{0,1:T(8,128)(2,1)} async-done(((bf16[256,1536]{0,1:T(8,128)(2,1)}), bf16[256,6144]{0,1:T(8,128)(2,1)}) %all-gather.3.cloned.1.call-update) | async-done | bytes 3145744 | tf_op jit(solution)/shard_map/all_gather | solution.py:128
  92.3 3.2 %copy.4.row_ref = bf16[256,6144]{1,0:T(8,128)(2,1)S(1)} copy(bf16[256,6144]{0,1:T(8,128)(2,1)} %all-gather.3.cloned.1.call-done) | data formatting | bytes 6291456 | tf_op jit(solution)/shard_map/all_gather | solution.py:128
  95.4 31.0 %shifted_rows.1 = bf16[16,256,6144]{2,1,0:T(8,128)(2,1)} custom-call(bf16[256,6144]{1,0:T(8,128)(2,1)S(1)} %copy.4.row_ref), custom_call_target="tpu_custom_call" | custom-call | tf_op jit(solution)/shard_map/shifted_rows/pallas_call | solution.py:30
  126.4 64.4 %lag_products.2.refs_2_ = f32[4,16,1024,128]{3,2,1,0:T(8,128)} custom-call(bf16[4096,6144]{1,0:T(8,128)(2,1)} %bitcast.7, bf16[6144,256]{1,0:T(8,128)(2,1)} %all-gather.5.cloned.1.call-done.refs_1_), custom_call_target="tpu_custom_call" | custom-call | tf_op jit(solution)/shard_map/lag_products/pallas_call | solution.py:94
  190.8 10.2 %collective-permute-done.2.refs_1_ = bf16[6144,256]{1,0:T(8,128)(2,1)} collective-permute-done((bf16[6144,256]{1,0:T(8,128)(2,1)}, bf16[6144,256]{1,0:T(8,128)(2,1)}, u32[]{:S(2)}, u32[]{:S(2)}) %collective-permute-start.2) | collective-permute-done | bytes 3145760 | tf_op jit(solution)/shard_map/ppermute | solution.py:110
  201.0 66.0 %lag_products.3 = f32[4,16,1024,128]{3,2,1,0:T(8,128)} custom-call(bf16[4096,6144]{1,0:T(8,128)(2,1)} %bitcast.8, bf16[6144,256]{1,0:T(8,128)(2,1)} %collective-permute-done.2.refs_1_, f32[4,16,1024,128]{3,2,1,0:T(8,128)} %lag_products.2.refs_2_), custom_call_target="tpu_custom_call", output_to_operand_aliasing={{}: (2, {})} | custom-call | tf_op jit(solution)/shard_map/lag_products/pallas_call | solution.py:94
Async XLA Ops:
  6.5 55.6 %all-gather.5.cloned.1.call-start = ((), (), s32[]{:S(2)}) async-start(), calls=%async_computation.1 | async-start | bytes 3932160 | tf_op jit(solution)/shard_map/all_gather | solution.py:137
  7.8 12.2 %collective-permute-start = (bf16[128,1536]{0,1:T(8,128)(2,1)S(1)}, bf16[128,1536]{0,1:T(8,128)(2,1)S(1)}, u32[]{:S(2)}, u32[]{:S(2)}) collective-permute-start(bf16[128,1536]{0,1:T(8,128)(2,1)S(1)} %bitcast.9), channel_id=1, source_target_pairs={{0,1},{1,0},{2,3},{3,2},{4,5},{5,4},{6,7},{7,6},{8,9},{9,8},{10,11... | collective-permute-start | bytes 1179656 | tf_op jit(solution)/shard_map/ppermute | solution.py:110
  21.0 10.3 %collective-permute-start.1 = (bf16[1536,128]{1,0:T(8,128)(2,1)S(1)}, bf16[1536,128]{1,0:T(8,128)(2,1)S(1)}, u32[]{:S(2)}, u32[]{:S(2)}) collective-permute-start(bf16[1536,128]{1,0:T(8,128)(2,1)S(1)} %bitcast.10), channel_id=1, source_target_pairs={{0,2},{2,0},{4,6},{6,4},{1,3},{3,1},{5,7},{7,5},{8,10},{10,8},{12,... | collective-permute-start | bytes 1179656 | tf_op jit(solution)/shard_map/ppermute | solution.py:131
  32.3 59.9 %all-gather.3.cloned.1.call-start = ((), (), s32[]{:S(2)}) async-start(), calls=%async_computation | async-start | bytes 3932160 | tf_op jit(solution)/shard_map/all_gather | solution.py:128
  62.2 138.9 %collective-permute-start.2 = (bf16[6144,256]{1,0:T(8,128)(2,1)}, bf16[6144,256]{1,0:T(8,128)(2,1)}, u32[]{:S(2)}, u32[]{:S(2)}) collective-permute-start(bf16[6144,256]{1,0:T(8,128)(2,1)} %all-gather.5.cloned.1.call-done.refs_1_), channel_id=1, source_target_pairs={{0,4},{2,6},{4,0},{6,2},{1,5},{3,7},{5,1},{7,3},{8,12},{10,14},{12... | collective-permute-start | bytes 9437192 | tf_op jit(solution)/shard_map/ppermute | solution.py:110
Sparse Core Ops, SparseCore 0:
  32.4 29.6 all-gather.4
  63.7 28.4 all-gather.2
